TPU v7x, 32 devices: a whole 2x2x4 slice. The times are simulated.
32 devices in a mesh: gx: 8 (over z, x), gy: 4 (over y, core).
Axes of the slice: x: 2, y: 2, z: 4, core: 2. Of those that a mesh axis runs over, the one named last changes fastest.
Arguments:
- right_side: float32 [4096, 128], P(('gx', 'gy'))
- compress: float32 [4096, 128], P(('gx', 'gy')), may hold values from 0.5 to 8
- block_fill: int32 [4096], P(('gx', 'gy')), may hold values from 32 to 128, as said below
- pair_home: int32 [12288], P(('gx', 'gy')), may hold values from 0 to 4095, as said below
- pair_far: int32 [12288], P(('gx', 'gy')), may hold values from 0 to 4095, as said below
- pair_count: int32 [32], P(('gx', 'gy')), may hold values from 1 to 384, as said below
- weights: bfloat16 [12288, 128, 128], P(('gx', 'gy')), may hold values from 0 to 0.015625
Outputs:
- solution_field: float32 [4096, 128], P(('gx', 'gy'))
- residual: float32 [4096, 128], P(('gx', 'gy'))
Inputs may be any that keep to these rules, and one draw needn't show every extreme that they name: `pair_home`: pair slot s names as first block a block of device s // 384, blocks of device d being d * 128 to d * 128 + 127, devices numbered gx major. `pair_far`: the second block belongs to the slot's device or to one of its eight neighbours on the periodic gx by gy grid of devices. `pair_count`: slots after a device's count are ignored; some devices hold 384. `block_fill`: slots after a block's fill are padding; some block holds 128.
All inputs are finite; a program needn't handle non-finite values.
Results may differ from a plain program's by a relative error of at most 0.015.
Values may be sent and summed in bfloat16 or wider, within the bound.
A program may use at most 64 MiB of HBM per device.

v0:
```python
import functools

import jax
import jax.numpy as jnp
from jax import lax
from jax.experimental import pallas as pl
from jax.experimental.pallas import tpu as pltpu
from jax.sharding import PartitionSpec as P

ITERS = 3
GROUP = 16
UNROLL = 3
MESH = pl.DeviceIdType.MESH
F32 = jnp.float32
BF16 = jnp.bfloat16


def matmul(a, b):
    return jnp.dot(a, b, preferred_element_type=F32)


def halves(value):
    high = value.astype(BF16)
    return high, (value - high.astype(F32)).astype(BF16)


def kernel(
    sizes,
    right_ref,
    compress_ref,
    fill_ref,
    home_ref,
    far_ref,
    count_ref,
    weights_hbm,
    x_ref,
    r_ref,
    wv,
    wt,
    onehot_home_t,
    onehot_home,
    onehot_far_t,
    onehot_far,
    mask,
    live,
    degree,
    gathered,
    rows_out,
    rows_sum,
    local,
    w_now,
    nearby,
    give,
    take,
    far_deg,
    give_deg,
    take_deg,
    red_y,
    red_x,
    load_sem,
    halo_send,
    halo_recv,
    ret_send,
    ret_recv,
    deg_send,
    deg_recv,
    ry_send,
    ry_recv,
    rx_send,
    rx_recv,
):
    n_x, n_y, chunks = sizes
    blocks, tile = right_ref.shape
    npairs = weights_hbm.shape[0]
    groups = npairs // GROUP
    per_chunk = npairs // chunks
    my_x = lax.axis_index("gx")
    my_y = lax.axis_index("gy")

    loads = [
        pltpu.make_async_copy(
            weights_hbm.at[pl.ds(i * per_chunk, per_chunk)],
            wv.at[pl.ds(i * per_chunk, per_chunk)],
            load_sem.at[i],
        )
        for i in range(chunks)
    ]
    for load in loads:
        load.start()

    def at(dx, dy):
        return (lax.rem(my_x + dx + n_x, n_x), lax.rem(my_y + dy + n_y, n_y))

    friends = {(dx % n_x, dy % n_y) for dx in (-1, 0, 1) for dy in (-1, 0, 1)}
    friends |= {(0, dy) for dy in range(n_y)} | {(dx, 0) for dx in range(n_x)}
    friends = sorted(friends - {(0, 0)})
    barrier = pltpu.get_barrier_semaphore()
    for dx, dy in friends:
        pl.semaphore_signal(barrier, inc=1, device_id=at(dx, dy), device_id_type=MESH)

    longer = 2 * lax.rem(my_x, 2) - 1
    order = [(longer, dy) for dy in (1, -1, 0)] + [(-longer, dy) for dy in (1, -1, 0)]
    order += [(0, 1), (0, -1)]
    around = [((dx + 1) * 3 + dy + 1, dx, dy) for dx, dy in order]

    def send(to, src, dst, ssem, rsem):
        return pltpu.make_async_remote_copy(
            src_ref=src,
            dst_ref=dst,
            send_sem=ssem,
            recv_sem=rsem,
            device_id=at(to[1], to[2]),
            device_id_type=MESH,
        )

    def halo(k):
        return [
            send(to, nearby.at[k, 4], nearby.at[k, 8 - to[0]], halo_send.at[k, to[0]], halo_recv.at[k, 8 - to[0]])
            for to in around
        ]

    def returns(k):
        return [
            send(to, give.at[k, to[0]], take.at[k, 8 - to[0]], ret_send.at[k, to[0]], ret_recv.at[k, 8 - to[0]])
            for to in around
        ]

    def degrees():
        return [
            send(to, give_deg.at[to[0]], take_deg.at[8 - to[0]], deg_send.at[to[0]], deg_recv.at[8 - to[0]])
            for to in around
        ]

    fill = jnp.broadcast_to(fill_ref[...].astype(F32), (tile, blocks)).T
    live_now = (lax.broadcasted_iota(jnp.int32, (blocks, tile), 1).astype(F32) < fill).astype(F32)
    live[...] = live_now
    nearby[0, 4] = (live_now * right_ref[...]).astype(BF16)

    pl.semaphore_wait(barrier, len(friends))
    for copy in halo(0):
        copy.start()

    keep = lax.broadcasted_iota(jnp.int32, (1, npairs), 1) < count_ref[0]
    home_row = jnp.broadcast_to(jnp.where(keep, home_ref[...], -1), (blocks, npairs))
    far_row = jnp.broadcast_to(jnp.where(keep, far_ref[...], -1), (blocks, npairs))
    which = lax.broadcasted_iota(jnp.int32, (blocks, npairs), 0)
    pick = jnp.where(which + (my_x * n_y + my_y) * blocks == home_row, 1.0, 0.0)
    onehot_home_t[...] = pick.astype(BF16)
    onehot_home[...] = pick.T.astype(BF16)
    for n in range(9):
        far_x, far_y = at(n // 3 - 1, n % 3 - 1)
        pick = jnp.where(which + (far_x * n_y + far_y) * blocks == far_row, 1.0, 0.0)
        onehot_far_t[n * blocks : (n + 1) * blocks, :] = pick.astype(BF16)
        onehot_far[:, n * blocks : (n + 1) * blocks] = pick.T.astype(BF16)
    for p in range(GROUP):
        own = lax.broadcasted_iota(jnp.int32, (GROUP, tile), 0) == p
        mask[:, p * tile : (p + 1) * tile] = jnp.where(own, 1.0, 0.0).astype(BF16)

    def rows(g):
        return pl.ds(pl.multiple_of(g * GROUP, GROUP), GROUP)

    def group_products(first, held, g, carry):
        x = gathered[rows(g), :]
        spread = mask[...]
        lhs = jnp.concatenate([x] * GROUP, axis=1) * spread
        if first:
            lhs = jnp.concatenate([lhs, spread], axis=0)
        out = matmul(lhs, held[pl.ds(g * GROUP, GROUP)].reshape(GROUP * tile, tile))
        rows_out[rows(g), :] = out[:GROUP].astype(BF16)
        if first:
            rows_sum[rows(g), :] = out[GROUP:]
        return carry

    def turned_products(g, carry):
        for p in range(GROUP):
            wt[g * GROUP + p] = wv[g * GROUP + p].T
        return group_products(True, wt, g, carry)

    def operate(k, field, during=None):
        first = k == 0
        gathered[...] = matmul(onehot_home[...], nearby[k, 4]).astype(BF16)
        if first:
            per = groups // chunks
            for i in range(chunks):
                loads[i].wait()
                lax.fori_loop(
                    i * per,
                    (i + 1) * per,
                    functools.partial(group_products, True, wv),
                    0,
                    unroll=UNROLL,
                )
            high, low = halves(rows_sum[...])
            for n in range(9):
                select = onehot_far_t[n * blocks : (n + 1) * blocks, :]
                far_deg[n] = matmul(select, high) + matmul(select, low)
                give_deg[n] = far_deg[n].astype(BF16)
            for copy in halo(k):
                copy.wait_recv()
        else:
            lax.fori_loop(
                0, groups, functools.partial(group_products, False, wv), 0, unroll=UNROLL
            )
        terms = rows_out[...]
        for n in (0, 1, 2, 6, 7, 8, 3, 5, 4):
            total = matmul(onehot_far_t[n * blocks : (n + 1) * blocks, :], terms)
            if first and n != 4:
                total -= far_deg[n] * nearby[k, n].astype(F32)
            if n == 4:
                local[...] = total
            else:
                give[k, n] = total.astype(BF16)
        for copy in returns(k):
            copy.start()
        if first:
            for copy in degrees():
                copy.start()
        if during is not None:
            during()
        if not first:
            for copy in halo(k):
                copy.wait_recv()
        gathered[...] = matmul(onehot_far[...], nearby[k].reshape(9 * blocks, tile)).astype(BF16)
        if first:
            lax.fori_loop(0, groups, turned_products, 0)
            high, low = halves(rows_sum[...])
            select = onehot_home_t[...]
            degree[...] = far_deg[4] + matmul(select, high) + matmul(select, low)
        else:
            lax.fori_loop(
                0, groups, functools.partial(group_products, False, wt), 0, unroll=UNROLL
            )
        total = local[...] + matmul(onehot_home_t[...], rows_out[...])
        if k == 1:
            for copy in degrees():
                copy.wait_recv()
            for n in (0, 1, 2, 3, 5, 6, 7, 8):
                degree[...] += take_deg[n].astype(F32)
        for copy in returns(k):
            copy.wait_recv()
        for n in (0, 1, 2, 3, 5, 6, 7, 8):
            total += take[k, n].astype(F32)
        pairs = degree[...] * nearby[k, 4].astype(F32) - total
        return compress_ref[...] * field + live[...] * pairs

    def sum_y(k):
        return [
            pltpu.make_async_remote_copy(
                src_ref=red_y.at[k, my_y],
                dst_ref=red_y.at[k, my_y],
                send_sem=ry_send.at[k, d],
                recv_sem=ry_recv.at[k, n_y - d],
                device_id=at(0, d),
                device_id_type=MESH,
            )
            for d in range(1, n_y)
        ]

    def sum_x(k):
        return [
            pltpu.make_async_remote_copy(
                src_ref=red_x.at[k, my_x],
                dst_ref=red_x.at[k, my_x],
                send_sem=rx_send.at[k, d],
                recv_sem=rx_recv.at[k, n_x - d],
                device_id=at(d, 0),
                device_id_type=MESH,
            )
            for d in range(1, n_x)
        ]

    def sums_start(k, residual, image):
        which_row = lax.broadcasted_iota(jnp.int32, (8, tile), 0)
        norm = jnp.sum(residual * residual, axis=0, keepdims=True)
        along = jnp.sum(residual * image, axis=0, keepdims=True)
        red_y[k, my_y] = jnp.where(which_row == 0, norm, jnp.where(which_row == 1, along, 0.0))
        for copy in sum_y(k):
            copy.start()

    def sums_middle(k):
        for copy in sum_y(k):
            copy.wait_recv()
        red_x[k, my_x] = jnp.sum(red_y[k], axis=0)
        for copy in sum_x(k):
            copy.start()

    def sums_end(k):
        for copy in sum_x(k):
            copy.wait_recv()
        totals = jnp.sum(jnp.sum(red_x[k], axis=0), axis=1, keepdims=True)
        return totals[0:1, :], totals[1:2, :]

    residual = right_ref[...]
    image = operate(0, residual)
    w_now[...] = image
    r_ref[...] = residual
    norm_before = alpha = direction = along = onward = None
    for k in range(ITERS):
        last = k + 1 == ITERS
        sums_start(k, r_ref[...], w_now[...])
        if not last:
            nearby[k + 1, 4] = (live[...] * w_now[...]).astype(BF16)
            for copy in halo(k + 1):
                copy.start()
            further = operate(k + 1, w_now[...], lambda: sums_middle(k))
        else:
            sums_middle(k)
        norm_now, product = sums_end(k)
        residual = r_ref[...]
        image = w_now[...]
        if k == 0:
            alpha = norm_now / product
            direction, along = residual, image
            x_ref[...] = alpha * direction
            if not last:
                onward = further
        else:
            ratio = norm_now / norm_before
            alpha = norm_now / (product - ratio * norm_now / alpha)
            direction = residual + ratio * direction
            along = image + ratio * along
            x_ref[...] += alpha * direction
            if not last:
                onward = further + ratio * onward
        norm_before = norm_now
        r_ref[...] = residual - alpha * along
        if not last:
            w_now[...] = image - alpha * onward

    for k in range(ITERS):
        for copy in halo(k) + returns(k) + sum_y(k) + sum_x(k):
            copy.wait_send()
    for copy in degrees():
        copy.wait_send()


def on_device(mesh_sizes, right_side, compress, block_fill, pair_home, pair_far, pair_count, weights):
    n_x, n_y = mesh_sizes
    blocks, tile = right_side.shape
    npairs = weights.shape[0]
    chunks = 4
    dma = pltpu.SemaphoreType.DMA
    vmem = pl.BlockSpec(memory_space=pltpu.VMEM)
    out = jax.ShapeDtypeStruct((blocks, tile), F32)
    return pl.pallas_call(
        functools.partial(kernel, (n_x, n_y, chunks)),
        out_shape=(out, out),
        in_specs=[vmem] * 5 + [pl.BlockSpec(memory_space=pltpu.SMEM), pl.BlockSpec(memory_space=pl.ANY)],
        out_specs=(vmem, vmem),
        scratch_shapes=[
            pltpu.VMEM((npairs, tile, tile), BF16),
            pltpu.VMEM((npairs, tile, tile), BF16),
            pltpu.VMEM((blocks, npairs), BF16),
            pltpu.VMEM((npairs, blocks), BF16),
            pltpu.VMEM((9 * blocks, npairs), BF16),
            pltpu.VMEM((npairs, 9 * blocks), BF16),
            pltpu.VMEM((GROUP, GROUP * tile), BF16),
            pltpu.VMEM((blocks, tile), F32),
            pltpu.VMEM((blocks, tile), F32),
            pltpu.VMEM((npairs, tile), BF16),
            pltpu.VMEM((npairs, tile), BF16),
            pltpu.VMEM((npairs, tile), F32),
            pltpu.VMEM((blocks, tile), F32),
            pltpu.VMEM((blocks, tile), F32),
            pltpu.VMEM((ITERS, 9, blocks, tile), BF16),
            pltpu.VMEM((ITERS, 9, blocks, tile), BF16),
            pltpu.VMEM((ITERS, 9, blocks, tile), BF16),
            pltpu.VMEM((9, blocks, tile), F32),
            pltpu.VMEM((9, blocks, tile), BF16),
            pltpu.VMEM((9, blocks, tile), BF16),
            pltpu.VMEM((ITERS, n_y, 8, tile), F32),
            pltpu.VMEM((ITERS, n_x, 8, tile), F32),
            dma((chunks,)),
            dma((ITERS, 9)),
            dma((ITERS, 9)),
            dma((ITERS, 9)),
            dma((ITERS, 9)),
            dma((9,)),
            dma((9,)),
            dma((ITERS, n_y)),
            dma((ITERS, n_y)),
            dma((ITERS, n_x)),
            dma((ITERS, n_x)),
        ],
        compiler_params=pltpu.CompilerParams(
            collective_id=0, has_side_effects=True, vmem_limit_bytes=56 * 1024 * 1024
        ),
    )(right_side, compress, block_fill[None], pair_home[None], pair_far[None], pair_count, weights)


def solution(mesh):
    return jax.shard_map(
        functools.partial(on_device, (mesh.shape["gx"], mesh.shape["gy"])),
        mesh=mesh,
        in_specs=(
            P(("gx", "gy"), None),
            P(("gx", "gy"), None),
            P(("gx", "gy")),
            P(("gx", "gy")),
            P(("gx", "gy")),
            P(("gx", "gy")),
            P(("gx", "gy"), None, None),
        ),
        out_specs=(P(("gx", "gy"), None), P(("gx", "gy"), None)),
        check_vma=False,
    )
```

profile of v0, /device:TPU:0, one launch (start us, length us, event | category | flops | bytes accessed | tf_op | source)
XLA Modules:
  0.0 62.5 jit_solution(250031665231118997)
XLA Ops:
  1.3 1.2 %broadcast_in_dim.10.home_ref = s32[1,384]{1,0:T(1,128)} reshape(s32[384]{0:T(512)} %param.10) | data formatting | bytes 3072 | tf_op jit(solution)/shard_map/broadcast_in_dim | solution.py:388
  2.5 1.2 %broadcast_in_dim.11.far_ref = s32[1,384]{1,0:T(1,128)} reshape(s32[384]{0:T(512)} %param.11) | data formatting | bytes 3072 | tf_op jit(solution)/shard_map/broadcast_in_dim | solution.py:388
  3.8 55.8 %shard_map.86 = (f32[128,128]{1,0:T(8,128)}, f32[128,128]{1,0:T(8,128)}) custom-call(f32[128,128]{1,0:T(8,128)} %right_ref.1, f32[128,128]{1,0:T(8,128)} %compress_ref.1, s32[1,128]{1,0:T(1,128)} %bitcast.1, s32[1,384]{1,0:T(1,128)} %broadcast_in_dim.10.home_ref, s32[1,384]{1,0:T(1,128)} %broadcast_in_dim.11.far_ref, s32[1]{0:T(128)S(6)} %copy.11.count_ref, ...), custom_call_target="tpu_custom_call" | custom-call | tf_op jit(solution)/shard_map/pallas_call | solution.py:345
  59.6 1.5 %copy.12 = f32[128,128]{1,0:T(8,128)} copy(f32[128,128]{1,0:T(8,128)} %get-tuple-element.4) | data formatting | bytes 131072
  61.1 1.5 %copy.13 = f32[128,128]{1,0:T(8,128)} copy(f32[128,128]{1,0:T(8,128)} %get-tuple-element.5) | data formatting | bytes 131072
where the time goes:
time: 62.9 us; the launch traced here: 62.5 us
  Pallas kernels  55.8 us (89%)
  local copies, waits for them, and re-layouts  5.44 us (9%)
  between operations  1.29 us (2%)
    pallas_call x1, Pallas kernels, on_device(): pl.pallas_call(functools.partial(kernel, (n_x, n_y, chunks)), out_shape=(...  55.8 us
    unnamed x2, local copies, waits for them, and re-layouts  2.95 us

commit v1 on v0

--- a/solution.py
+++ b/solution.py
@@ -9,7 +9,7 @@
 
 ITERS = 3
 GROUP = 16
-UNROLL = 3
+UNROLL = 6
 MESH = pl.DeviceIdType.MESH
 F32 = jnp.float32
 BF16 = jnp.bfloat16
@@ -26,15 +26,20 @@
 
 def kernel(
     sizes,
+    right_hbm,
+    compress_hbm,
+    fill_hbm,
+    home_hbm,
+    far_hbm,
+    count_ref,
+    weights_hbm,
+    x_ref,
+    r_ref,
     right_ref,
     compress_ref,
     fill_ref,
     home_ref,
     far_ref,
-    count_ref,
-    weights_hbm,
-    x_ref,
-    r_ref,
     wv,
     wt,
     onehot_home_t,
@@ -49,6 +54,9 @@
     rows_sum,
     local,
     w_now,
+    s_now,
+    d_now,
+    onward,
     nearby,
     give,
     take,
@@ -58,6 +66,7 @@
     red_y,
     red_x,
     load_sem,
+    in_sem,
     halo_send,
     halo_recv,
     ret_send,
@@ -70,13 +79,37 @@
     rx_recv,
 ):
     n_x, n_y, chunks = sizes
-    blocks, tile = right_ref.shape
+    blocks, tile = right_hbm.shape
     npairs = weights_hbm.shape[0]
     groups = npairs // GROUP
     per_chunk = npairs // chunks
     my_x = lax.axis_index("gx")
     my_y = lax.axis_index("gy")
 
+    def at(dx, dy):
+        return (lax.rem(my_x + dx + n_x, n_x), lax.rem(my_y + dy + n_y, n_y))
+
+    friends = {(dx % n_x, dy % n_y) for dx in (-1, 0, 1) for dy in (-1, 0, 1)}
+    friends |= {(0, dy) for dy in range(n_y)} | {(dx, 0) for dx in range(n_x)}
+    friends = sorted(friends - {(0, 0)})
+    barrier = pltpu.get_barrier_semaphore()
+    for dx, dy in friends:
+        pl.semaphore_signal(barrier, inc=1, device_id=at(dx, dy), device_id_type=MESH)
+
+    inputs = [
+        pltpu.make_async_copy(src, dst, in_sem.at[i])
+        for i, (src, dst) in enumerate(
+            (
+                (fill_hbm, fill_ref),
+                (right_hbm, right_ref),
+                (home_hbm, home_ref),
+                (far_hbm, far_ref),
+                (compress_hbm, compress_ref),
+            )
+        )
+    ]
+    for copy in inputs:
+        copy.start()
     loads = [
         pltpu.make_async_copy(
             weights_hbm.at[pl.ds(i * per_chunk, per_chunk)],
@@ -88,16 +121,6 @@
     for load in loads:
         load.start()
 
-    def at(dx, dy):
-        return (lax.rem(my_x + dx + n_x, n_x), lax.rem(my_y + dy + n_y, n_y))
-
-    friends = {(dx % n_x, dy % n_y) for dx in (-1, 0, 1) for dy in (-1, 0, 1)}
-    friends |= {(0, dy) for dy in range(n_y)} | {(dx, 0) for dx in range(n_x)}
-    friends = sorted(friends - {(0, 0)})
-    barrier = pltpu.get_barrier_semaphore()
-    for dx, dy in friends:
-        pl.semaphore_signal(barrier, inc=1, device_id=at(dx, dy), device_id_type=MESH)
-
     longer = 2 * lax.rem(my_x, 2) - 1
     order = [(longer, dy) for dy in (1, -1, 0)] + [(-longer, dy) for dy in (1, -1, 0)]
     order += [(0, 1), (0, -1)]
@@ -131,6 +154,8 @@
             for to in around
         ]
 
+    for copy in inputs[:2]:
+        copy.wait()
     fill = jnp.broadcast_to(fill_ref[...].astype(F32), (tile, blocks)).T
     live_now = (lax.broadcasted_iota(jnp.int32, (blocks, tile), 1).astype(F32) < fill).astype(F32)
     live[...] = live_now
@@ -140,6 +165,8 @@
     for copy in halo(0):
         copy.start()
 
+    for copy in inputs[2:]:
+        copy.wait()
     keep = lax.broadcasted_iota(jnp.int32, (1, npairs), 1) < count_ref[0]
     home_row = jnp.broadcast_to(jnp.where(keep, home_ref[...], -1), (blocks, npairs))
     far_row = jnp.broadcast_to(jnp.where(keep, far_ref[...], -1), (blocks, npairs))
@@ -159,37 +186,38 @@
     def rows(g):
         return pl.ds(pl.multiple_of(g * GROUP, GROUP), GROUP)
 
-    def group_products(first, held, g, carry):
+    def group_products(first, turn, held, g, carry):
         x = gathered[rows(g), :]
         spread = mask[...]
         lhs = jnp.concatenate([x] * GROUP, axis=1) * spread
         if first:
             lhs = jnp.concatenate([lhs, spread], axis=0)
-        out = matmul(lhs, held[pl.ds(g * GROUP, GROUP)].reshape(GROUP * tile, tile))
+        if turn:
+            rhs = jnp.concatenate([held[g * GROUP + p] for p in range(GROUP)], axis=1)
+            out = lax.dot_general(lhs, rhs, (((1,), (1,)), ((), ())), preferred_element_type=F32)
+        else:
+            out = matmul(lhs, held[pl.ds(g * GROUP, GROUP)].reshape(GROUP * tile, tile))
         rows_out[rows(g), :] = out[:GROUP].astype(BF16)
         if first:
             rows_sum[rows(g), :] = out[GROUP:]
         return carry
 
-    def turned_products(g, carry):
+    def products(first, turn, held, start, stop, unroll=UNROLL):
+        lax.fori_loop(start, stop, functools.partial(group_products, first, turn, held), 0, unroll=unroll)
+
+    def turn_tiles(g, carry):
         for p in range(GROUP):
             wt[g * GROUP + p] = wv[g * GROUP + p].T
-        return group_products(True, wt, g, carry)
-
-    def operate(k, field, during=None):
+        return carry
+
+    def operate(k, field, during=None, late=None):
         first = k == 0
         gathered[...] = matmul(onehot_home[...], nearby[k, 4]).astype(BF16)
         if first:
             per = groups // chunks
             for i in range(chunks):
                 loads[i].wait()
-                lax.fori_loop(
-                    i * per,
-                    (i + 1) * per,
-                    functools.partial(group_products, True, wv),
-                    0,
-                    unroll=UNROLL,
-                )
+                products(True, False, wv, i * per, (i + 1) * per)
             high, low = halves(rows_sum[...])
             for n in range(9):
                 select = onehot_far_t[n * blocks : (n + 1) * blocks, :]
@@ -198,9 +226,7 @@
             for copy in halo(k):
                 copy.wait_recv()
         else:
-            lax.fori_loop(
-                0, groups, functools.partial(group_products, False, wv), 0, unroll=UNROLL
-            )
+            products(False, False, wv, 0, groups)
         terms = rows_out[...]
         for n in (0, 1, 2, 6, 7, 8, 3, 5, 4):
             total = matmul(onehot_far_t[n * blocks : (n + 1) * blocks, :], terms)
@@ -217,20 +243,31 @@
                 copy.start()
         if during is not None:
             during()
+        if k == 1:
+            lax.fori_loop(groups // 2, groups, turn_tiles, 0, unroll=2)
         if not first:
             for copy in halo(k):
                 copy.wait_recv()
         gathered[...] = matmul(onehot_far[...], nearby[k].reshape(9 * blocks, tile)).astype(BF16)
-        if first:
-            lax.fori_loop(0, groups, turned_products, 0)
+        if late is not None:
+            across = jnp.sum(terms.astype(F32) * gathered[...].astype(F32), axis=0, keepdims=True)
+            own = nearby[k, 4].astype(F32)
+            within = jnp.sum(
+                compress_ref[...] * field * field + degree[...] * own * own, axis=0, keepdims=True
+            )
+            late(within - 2.0 * across)
+        if first:
+            products(True, True, wv, 0, groups, 3)
             high, low = halves(rows_sum[...])
             select = onehot_home_t[...]
             degree[...] = far_deg[4] + matmul(select, high) + matmul(select, low)
         else:
-            lax.fori_loop(
-                0, groups, functools.partial(group_products, False, wt), 0, unroll=UNROLL
-            )
+            products(False, False, wt, 0, groups)
         total = local[...] + matmul(onehot_home_t[...], rows_out[...])
+        if late is not None:
+            sums_middle(k)
+        if first:
+            lax.fori_loop(0, groups // 2, turn_tiles, 0, unroll=2)
         if k == 1:
             for copy in degrees():
                 copy.wait_recv()
@@ -269,11 +306,15 @@
             for d in range(1, n_x)
         ]
 
-    def sums_start(k, residual, image):
+    def column(value):
+        return jnp.sum(value, axis=0, keepdims=True)
+
+    def sums_start(k, terms):
         which_row = lax.broadcasted_iota(jnp.int32, (8, tile), 0)
-        norm = jnp.sum(residual * residual, axis=0, keepdims=True)
-        along = jnp.sum(residual * image, axis=0, keepdims=True)
-        red_y[k, my_y] = jnp.where(which_row == 0, norm, jnp.where(which_row == 1, along, 0.0))
+        packed = jnp.zeros((8, tile), F32)
+        for i, term in enumerate(terms):
+            packed = jnp.where(which_row == i, term, packed)
+        red_y[k, my_y] = packed
         for copy in sum_y(k):
             copy.start()
 
@@ -288,44 +329,67 @@
         for copy in sum_x(k):
             copy.wait_recv()
         totals = jnp.sum(jnp.sum(red_x[k], axis=0), axis=1, keepdims=True)
-        return totals[0:1, :], totals[1:2, :]
+        return [totals[i : i + 1, :] for i in range(8)]
 
     residual = right_ref[...]
     image = operate(0, residual)
+    r_ref[...] = residual
     w_now[...] = image
-    r_ref[...] = residual
-    norm_before = alpha = direction = along = onward = None
-    for k in range(ITERS):
-        last = k + 1 == ITERS
-        sums_start(k, r_ref[...], w_now[...])
-        if not last:
-            nearby[k + 1, 4] = (live[...] * w_now[...]).astype(BF16)
-            for copy in halo(k + 1):
-                copy.start()
-            further = operate(k + 1, w_now[...], lambda: sums_middle(k))
+    sums_start(0, (column(residual * residual), column(residual * image)))
+    s_now[...] = image
+    nearby[1, 4] = (live[...] * image).astype(BF16)
+    for copy in halo(1):
+        copy.start()
+    onward[...] = operate(1, image, lambda: sums_middle(0))
+    norm_now, product = sums_end(0)[:2]
+    alpha = norm_now / product
+    x_ref[...] = alpha * residual
+    d_now[...] = residual
+    residual = residual - alpha * s_now[...]
+    image = image - alpha * onward[...]
+    for k in range(1, ITERS - 1):
+        final = k + 2 == ITERS
+        r_ref[...] = residual
+        w_now[...] = image
+        sums_start(k, (column(residual * residual), column(residual * image)))
+        nearby[k + 1, 4] = (live[...] * image).astype(BF16)
+        for copy in halo(k + 1):
+            copy.start()
+        coefficients = []
+
+        def advance():
+            norm_next, product = sums_end(k)[:2]
+            ratio = norm_next / norm_now
+            alpha_next = norm_next / (product - ratio * norm_next / alpha)
+            coefficients.extend((norm_next, ratio, alpha_next))
+            d_now[...] = r_ref[...] + ratio * d_now[...]
+            s_now[...] = w_now[...] + ratio * s_now[...]
+            x_ref[...] += alpha_next * d_now[...]
+            r_ref[...] -= alpha_next * s_now[...]
+
+        def early(energy):
+            advance()
+            r_next, w, q = r_ref[...], w_now[...], onward[...]
+            sums_start(
+                k + 1,
+                (column(r_next * r_next), column(r_next * w), column(r_next * q), column(w * w), column(q * w), energy),
+            )
+
+        if final:
+            further = operate(k + 1, image, lambda: sums_middle(k), early)
         else:
-            sums_middle(k)
-        norm_now, product = sums_end(k)
+            further = operate(k + 1, image, lambda: sums_middle(k))
+            advance()
+        norm_now, ratio, alpha = coefficients
+        onward[...] = further + ratio * onward[...]
         residual = r_ref[...]
-        image = w_now[...]
-        if k == 0:
-            alpha = norm_now / product
-            direction, along = residual, image
-            x_ref[...] = alpha * direction
-            if not last:
-                onward = further
-        else:
-            ratio = norm_now / norm_before
-            alpha = norm_now / (product - ratio * norm_now / alpha)
-            direction = residual + ratio * direction
-            along = image + ratio * along
-            x_ref[...] += alpha * direction
-            if not last:
-                onward = further + ratio * onward
-        norm_before = norm_now
-        r_ref[...] = residual - alpha * along
-        if not last:
-            w_now[...] = image - alpha * onward
+        image = w_now[...] - alpha * onward[...]
+    norm_last, r_w, r_q, w_w, q_w, energy = sums_end(ITERS - 1)[:6]
+    product = r_w - alpha * (w_w - alpha * (energy + ratio * q_w)) - alpha * ratio * r_q
+    ratio = norm_last / norm_now
+    alpha = norm_last / (product - ratio * norm_last / alpha)
+    x_ref[...] += alpha * (residual + ratio * d_now[...])
+    r_ref[...] = residual - alpha * (image + ratio * s_now[...])
 
     for k in range(ITERS):
         for copy in halo(k) + returns(k) + sum_y(k) + sum_x(k):
@@ -345,9 +409,15 @@
     return pl.pallas_call(
         functools.partial(kernel, (n_x, n_y, chunks)),
         out_shape=(out, out),
-        in_specs=[vmem] * 5 + [pl.BlockSpec(memory_space=pltpu.SMEM), pl.BlockSpec(memory_space=pl.ANY)],
+        in_specs=[pl.BlockSpec(memory_space=pl.ANY)] * 5
+        + [pl.BlockSpec(memory_space=pltpu.SMEM), pl.BlockSpec(memory_space=pl.ANY)],
         out_specs=(vmem, vmem),
         scratch_shapes=[
+            pltpu.VMEM((blocks, tile), F32),
+            pltpu.VMEM((blocks, tile), F32),
+            pltpu.VMEM((1, blocks), jnp.int32),
+            pltpu.VMEM((1, npairs), jnp.int32),
+            pltpu.VMEM((1, npairs), jnp.int32),
             pltpu.VMEM((npairs, tile, tile), BF16),
             pltpu.VMEM((npairs, tile, tile), BF16),
             pltpu.VMEM((blocks, npairs), BF16),
@@ -360,6 +430,9 @@
             pltpu.VMEM((npairs, tile), BF16),
             pltpu.VMEM((npairs, tile), BF16),
             pltpu.VMEM((npairs, tile), F32),
+            pltpu.VMEM((blocks, tile), F32),
+            pltpu.VMEM((blocks, tile), F32),
+            pltpu.VMEM((blocks, tile), F32),
             pltpu.VMEM((blocks, tile), F32),
             pltpu.VMEM((blocks, tile), F32),
             pltpu.VMEM((ITERS, 9, blocks, tile), BF16),
@@ -371,6 +444,7 @@
             pltpu.VMEM((ITERS, n_y, 8, tile), F32),
             pltpu.VMEM((ITERS, n_x, 8, tile), F32),
             dma((chunks,)),
+            dma((5,)),
             dma((ITERS, 9)),
             dma((ITERS, 9)),
             dma((ITERS, 9)),

time: 62.9 us -> 59.3 us (0.943)
  Pallas kernels: 55.8 us -> 52.4 us
    pallas_call x1, Pallas kernels: 55.8 us -> 52.4 us  [on_device(): pl.pallas_call(functools.partial(kernel, (n_x, n_y, chunks)), out_shape=(...]
where the time goes in v1:
time: 59.3 us; the launch traced here: 59.1 us
  Pallas kernels  52.4 us (88%)
  local copies, waits for them, and re-layouts  5.44 us (9%)
  between operations  1.29 us (2%)
    pallas_call x1, Pallas kernels, on_device(): pl.pallas_call(functools.partial(kernel, (n_x, n_y, chunks)), out_shape=(...  52.4 us
    unnamed x2, local copies, waits for them, and re-layouts  2.95 us
    broadcast_in_dim x1, local copies, waits for them, and re-layouts, on_device(): pair_home[None]  1.25 us
    broadcast_in_dim x1, local copies, waits for them, and re-layouts, on_device(): pair_far[None]  1.24 us

profile of v1, /device:TPU:0, one launch (start us, length us, event | category | flops | bytes accessed | tf_op | source)
XLA Modules:
  0.0 59.1 jit_solution(9513826698503394370)
XLA Ops:
  1.3 1.2 %broadcast_in_dim.10.home_hbm = s32[1,384]{1,0:T(1,128)} reshape(s32[384]{0:T(512)} %param.10) | data formatting | bytes 3072 | tf_op jit(solution)/shard_map/broadcast_in_dim | solution.py:462
  2.5 1.2 %broadcast_in_dim.11.far_hbm = s32[1,384]{1,0:T(1,128)} reshape(s32[384]{0:T(512)} %param.11) | data formatting | bytes 3072 | tf_op jit(solution)/shard_map/broadcast_in_dim | solution.py:462
  3.8 52.4 %shard_map.86 = (f32[128,128]{1,0:T(8,128)}, f32[128,128]{1,0:T(8,128)}) custom-call(f32[128,128]{1,0:T(8,128)} %right_hbm.1, f32[128,128]{1,0:T(8,128)} %compress_hbm.1, s32[1,128]{1,0:T(1,128)} %bitcast.1, s32[1,384]{1,0:T(1,128)} %broadcast_in_dim.10.home_hbm, s32[1,384]{1,0:T(1,128)} %broadcast_in_dim.11.far_hbm, s32[1]{0:T(128)S(6)} %copy.11.count_ref, ...), custom_call_target="tpu_custom_call" | custom-call | tf_op jit(solution)/shard_map/pallas_call | solution.py:409
  56.1 1.5 %copy.12 = f32[128,128]{1,0:T(8,128)} copy(f32[128,128]{1,0:T(8,128)} %get-tuple-element.4) | data formatting | bytes 131072
  57.6 1.5 %copy.13 = f32[128,128]{1,0:T(8,128)} copy(f32[128,128]{1,0:T(8,128)} %get-tuple-element.5) | data formatting | bytes 131072

commit v2 on v1

--- a/solution.py
+++ b/solution.py
@@ -100,10 +100,10 @@
         pltpu.make_async_copy(src, dst, in_sem.at[i])
         for i, (src, dst) in enumerate(
             (
-                (fill_hbm, fill_ref),
+                (fill_hbm, fill_ref.at[0]),
                 (right_hbm, right_ref),
-                (home_hbm, home_ref),
-                (far_hbm, far_ref),
+                (home_hbm, home_ref.at[0]),
+                (far_hbm, far_ref.at[0]),
                 (compress_hbm, compress_ref),
             )
         )
@@ -118,8 +118,7 @@
         )
         for i in range(chunks)
     ]
-    for load in loads:
-        load.start()
+    loads[0].start()
 
     longer = 2 * lax.rem(my_x, 2) - 1
     order = [(longer, dy) for dy in (1, -1, 0)] + [(-longer, dy) for dy in (1, -1, 0)]
@@ -136,11 +135,40 @@
             device_id_type=MESH,
         )
 
+    def place(dx, dy):
+        return (dx + 1) * 3 + dy + 1
+
     def halo(k):
         return [
-            send(to, nearby.at[k, 4], nearby.at[k, 8 - to[0]], halo_send.at[k, to[0]], halo_recv.at[k, 8 - to[0]])
-            for to in around
-        ]
+            send((n, dx, dy), nearby.at[k, 4], nearby.at[k, 8 - n], halo_send.at[k, n], halo_recv.at[k, 8 - n])
+            for n, dx, dy in ((place(dx, dy), dx, dy) for dx, dy in ((longer, 0), (-longer, 0), (0, 1), (0, -1)))
+        ]
+
+    def relay(k, dx):
+        held = place(dx, 0)
+        return [
+            send(
+                (0, 0, dy),
+                nearby.at[k, held],
+                nearby.at[k, place(dx, -dy)],
+                halo_send.at[k, place(dx, dy)],
+                halo_recv.at[k, place(dx, -dy)],
+            )
+            for dy in (1, -1)
+        ]
+
+    def halo_pass_on(k):
+        for dx in (-longer, longer):
+            arrived(k, place(dx, 0)).wait_recv()
+            for copy in relay(k, dx):
+                copy.start()
+
+    def halo_finish(k):
+        for n in (0, 2, 6, 8, 3, 5):
+            arrived(k, n).wait_recv()
+
+    def arrived(k, n):
+        return send((0, 0, 1), nearby.at[k, 4], nearby.at[k, n], halo_send.at[k, 4], halo_recv.at[k, n])
 
     def returns(k):
         return [
@@ -148,14 +176,35 @@
             for to in around
         ]
 
-    def degrees():
-        return [
-            send(to, give_deg.at[to[0]], take_deg.at[8 - to[0]], deg_send.at[to[0]], deg_recv.at[8 - to[0]])
-            for to in around
-        ]
-
-    for copy in inputs[:2]:
+    def degrees_y():
+        return [
+            send(
+                (0, 0, dy),
+                give_deg.at[place(dx, dy)],
+                take_deg.at[place(dx, -dy)],
+                deg_send.at[place(dx, dy)],
+                deg_recv.at[place(dx, -dy)],
+            )
+            for dx in (1, -1, 0)
+            for dy in (1, -1)
+        ]
+
+    def degrees_x():
+        return [
+            send(
+                (0, dx, 0),
+                give_deg.at[place(dx, 0)],
+                take_deg.at[place(-dx, 0)],
+                deg_send.at[place(dx, 0)],
+                deg_recv.at[place(-dx, 0)],
+            )
+            for dx in (1, -1)
+        ]
+
+    for copy in inputs[:4]:
         copy.wait()
+    for load in loads[1:]:
+        load.start()
     fill = jnp.broadcast_to(fill_ref[...].astype(F32), (tile, blocks)).T
     live_now = (lax.broadcasted_iota(jnp.int32, (blocks, tile), 1).astype(F32) < fill).astype(F32)
     live[...] = live_now
@@ -165,8 +214,6 @@
     for copy in halo(0):
         copy.start()
 
-    for copy in inputs[2:]:
-        copy.wait()
     keep = lax.broadcasted_iota(jnp.int32, (1, npairs), 1) < count_ref[0]
     home_row = jnp.broadcast_to(jnp.where(keep, home_ref[...], -1), (blocks, npairs))
     far_row = jnp.broadcast_to(jnp.where(keep, far_ref[...], -1), (blocks, npairs))
@@ -218,15 +265,19 @@
             for i in range(chunks):
                 loads[i].wait()
                 products(True, False, wv, i * per, (i + 1) * per)
+            halo_pass_on(k)
             high, low = halves(rows_sum[...])
             for n in range(9):
                 select = onehot_far_t[n * blocks : (n + 1) * blocks, :]
                 far_deg[n] = matmul(select, high) + matmul(select, low)
-                give_deg[n] = far_deg[n].astype(BF16)
-            for copy in halo(k):
-                copy.wait_recv()
+                if n % 3 != 1:
+                    give_deg[n] = far_deg[n].astype(BF16)
+            lax.fori_loop(0, groups // 2, turn_tiles, 0, unroll=2)
+            halo_finish(k)
         else:
             products(False, False, wv, 0, groups)
+        if during is not None:
+            during()
         terms = rows_out[...]
         for n in (0, 1, 2, 6, 7, 8, 3, 5, 4):
             total = matmul(onehot_far_t[n * blocks : (n + 1) * blocks, :], terms)
@@ -236,18 +287,20 @@
                 local[...] = total
             else:
                 give[k, n] = total.astype(BF16)
-        for copy in returns(k):
+        outgoing = returns(k)
+        for copy in outgoing[:6]:
+            copy.start()
+        if not first:
+            halo_pass_on(k)
+        for copy in outgoing[6:]:
             copy.start()
         if first:
-            for copy in degrees():
+            for copy in degrees_y():
                 copy.start()
-        if during is not None:
-            during()
         if k == 1:
             lax.fori_loop(groups // 2, groups, turn_tiles, 0, unroll=2)
         if not first:
-            for copy in halo(k):
-                copy.wait_recv()
+            halo_finish(k)
         gathered[...] = matmul(onehot_far[...], nearby[k].reshape(9 * blocks, tile)).astype(BF16)
         if late is not None:
             across = jnp.sum(terms.astype(F32) * gathered[...].astype(F32), axis=0, keepdims=True)
@@ -257,21 +310,31 @@
             )
             late(within - 2.0 * across)
         if first:
-            products(True, True, wv, 0, groups, 3)
+            products(True, False, wt, 0, groups // 2)
+            products(True, True, wv, groups // 2, groups, 3)
             high, low = halves(rows_sum[...])
             select = onehot_home_t[...]
             degree[...] = far_deg[4] + matmul(select, high) + matmul(select, low)
+            for copy in degrees_y():
+                copy.wait_recv()
+            for dx in (1, -1):
+                both = take_deg[place(dx, 1)].astype(F32) + take_deg[place(dx, -1)].astype(F32)
+                give_deg[place(dx, 0)] = (far_deg[place(dx, 0)] + both).astype(BF16)
+            for copy in degrees_x():
+                copy.start()
+        elif late is None:
+            products(False, False, wt, 0, groups)
         else:
-            products(False, False, wt, 0, groups)
+            products(False, False, wt, 0, groups * 3 // 4)
+            sums_middle(k)
+            products(False, False, wt, groups * 3 // 4, groups)
         total = local[...] + matmul(onehot_home_t[...], rows_out[...])
-        if late is not None:
-            sums_middle(k)
         if first:
-            lax.fori_loop(0, groups // 2, turn_tiles, 0, unroll=2)
+            inputs[4].wait()
         if k == 1:
-            for copy in degrees():
+            for copy in degrees_x():
                 copy.wait_recv()
-            for n in (0, 1, 2, 3, 5, 6, 7, 8):
+            for n in (1, 3, 5, 7):
                 degree[...] += take_deg[n].astype(F32)
         for copy in returns(k):
             copy.wait_recv()
@@ -392,10 +455,15 @@
     r_ref[...] = residual - alpha * (image + ratio * s_now[...])
 
     for k in range(ITERS):
-        for copy in halo(k) + returns(k) + sum_y(k) + sum_x(k):
+        for copy in halo(k) + relay(k, 1) + relay(k, -1) + returns(k) + sum_y(k) + sum_x(k):
             copy.wait_send()
-    for copy in degrees():
+    for copy in degrees_y() + degrees_x():
         copy.wait_send()
+
+
+def hand_over(x_in, r_in, x_out, r_out):
+    x_out[...] = x_in[...]
+    r_out[...] = r_in[...]
 
 
 def on_device(mesh_sizes, right_side, compress, block_fill, pair_home, pair_far, pair_count, weights):
@@ -406,7 +474,7 @@
     dma = pltpu.SemaphoreType.DMA
     vmem = pl.BlockSpec(memory_space=pltpu.VMEM)
     out = jax.ShapeDtypeStruct((blocks, tile), F32)
-    return pl.pallas_call(
+    x, r = pl.pallas_call(
         functools.partial(kernel, (n_x, n_y, chunks)),
         out_shape=(out, out),
         in_specs=[pl.BlockSpec(memory_space=pl.ANY)] * 5
@@ -459,7 +527,8 @@
         compiler_params=pltpu.CompilerParams(
             collective_id=0, has_side_effects=True, vmem_limit_bytes=56 * 1024 * 1024
         ),
-    )(right_side, compress, block_fill[None], pair_home[None], pair_far[None], pair_count, weights)
+    )(right_side, compress, block_fill, pair_home, pair_far, pair_count, weights)
+    return pl.pallas_call(hand_over, out_shape=(out, out), in_specs=[vmem] * 2, out_specs=(vmem, vmem))(x, r)
 
 
 def solution(mesh):

time: 59.3 us -> 52.1 us (0.88)
  local copies, waits for them, and re-layouts: 5.44 us -> 0 us
  Pallas kernels: 52.4 us -> 50.6 us
    pallas_call x1, Pallas kernels: 52.4 us -> 49.1 us  [on_device(): pl.pallas_call(functools.partial(kernel, (n_x, n_y, chunks)), out_shape=(...]
    unnamed x2 -> x0, local copies, waits for them, and re-layouts: 2.95 us -> none
    broadcast_in_dim x2 -> x0, local copies, waits for them, and re-layouts: 2.49 us -> none  [the longest x1 1.25 us: on_device(): pair_home[None]]
    pallas_call x0 -> x1, Pallas kernels: none -> 1.53 us  [on_device(): pl.pallas_call(hand_over, out_shape=(out, out), in_specs=[vmem] * 2, out_...]
where the time goes in v2:
time: 52.1 us; the launch traced here: 51.9 us
  Pallas kernels  50.6 us (97%)
  between operations  1.29 us (2%)
    pallas_call x1, Pallas kernels, on_device(): pl.pallas_call(functools.partial(kernel, (n_x, n_y, chunks)), out_shape=(...  49.1 us
    pallas_call x1, Pallas kernels, on_device(): pl.pallas_call(hand_over, out_shape=(out, out), in_specs=[vmem] * 2, out_...  1.53 us

profile of v2, /device:TPU:0, one launch (start us, length us, event | category | flops | bytes accessed | tf_op | source)
XLA Modules:
  0.0 51.9 jit_solution(15433669829498094170)
XLA Ops:
  1.3 49.1 %shard_map.86 = (f32[128,128]{1,0:T(8,128)}, f32[128,128]{1,0:T(8,128)}) custom-call(f32[128,128]{1,0:T(8,128)} %right_hbm.1, f32[128,128]{1,0:T(8,128)} %compress_hbm.1, s32[128]{0:T(128)} %fill_hbm.1, s32[384]{0:T(512)} %home_hbm.1, s32[384]{0:T(512)} %far_hbm.1, s32[1]{0:T(128)S(6)} %copy.9.count_ref, bf16[384,128,128]{2,1,0:T(8,128)(2,1)} %weights_hbm.1), custom_call_target="tpu_custom_call" | custom-call | tf_op jit(solution)/shard_map/pallas_call | solution.py:477
  50.4 1.5 %shard_map.87 = (f32[128,128]{1,0:T(8,128)}, f32[128,128]{1,0:T(8,128)}) custom-call(f32[128,128]{1,0:T(8,128)} %get-tuple-element.4.x_in, f32[128,128]{1,0:T(8,128)} %get-tuple-element.5.r_in), custom_call_target="tpu_custom_call" | custom-call | tf_op jit(solution)/shard_map/pallas_call | solution.py:531
